TPU v7x, 256 devices: a whole 4x4x8 slice. The times are simulated.
256 devices in a mesh: heads: 16 (over x_lo, y, core), keys: 16 (over z, x_hi).
Axes of the slice: x: 4 (x_hi: 2, x_lo: 2; x = x_hi * 2 + x_lo), y: 4, z: 8, core: 2. Of those that a mesh axis runs over, the one named last changes fastest.
Arguments:
- main_query: bfloat16 [256, 128, 576], P(None, 'heads'), may hold values from -5 to 5
- latent_keys: bfloat16 [32768, 576], P('keys'), may hold values from -16 to 16
- index_query: bfloat16 [256, 64, 128], P('heads'), may hold values from -1 to 1
- index_keys: bfloat16 [32768, 128], P('keys'), may hold values from -20 to 20
- index_weight: float32 [256, 64], P('heads'), may hold values from -0.15 to 1
- query_pos: int32 [256], replicated, may hold values from 4096 to 32767, as said below
- kl_weight: float32 [256], P('heads'), may hold values from 2 to 16
Outputs:
- index_query_grad: float32 [256, 64, 128], P('heads')
- index_key_grad: float32 [32768, 128], P('keys')
- index_weight_grad: float32 [256, 64], P('heads')
Inputs may be any that keep to these rules, and one draw needn't show every extreme that they name: Query q sees the keys at positions 0 to query_pos[q]; some query sees all 32768 keys and some sees exactly the first 4097.
All inputs are finite; a program needn't handle non-finite values.
Results may differ from a plain program's by a relative error of at most 0.005.
Values sent between devices are 32-bit elements; how exact they have to be, the bound alone decides.
A program may use at most 128 MiB of HBM per device.

v0:
```python
import jax
import jax.numpy as jnp
from jax import lax
from jax.sharding import PartitionSpec as P

H = 128
softmax_scale = 192.0 ** (-0.5)
masked_fill = -1e30


def contract_last(left_side, right_side):
    return lax.dot_general(
        left_side, right_side, (((1,), (1,)), ((), ())), preferred_element_type=jnp.float32
    )


def shards(main_query, latent_keys, index_query, index_keys, index_weight, query_pos, kl_weight):
    query_count, head_local, feature_width = main_query.shape
    key_local = latent_keys.shape[0]
    row_local, index_heads, index_width = index_query.shape
    key_first = lax.axis_index("keys") * key_local
    key_index = key_first + lax.iota(jnp.int32, key_local)
    visible = key_index[None, :] <= query_pos[:, None]
    row_first = lax.axis_index("heads") * row_local
    row_pos = lax.dynamic_slice_in_dim(query_pos, row_first, row_local)
    row_visible = key_index[None, :] <= row_pos[:, None]
    main_scores = contract_last(
        main_query.reshape(query_count * head_local, feature_width), latent_keys
    )
    main_scores = main_scores.reshape(query_count, head_local, key_local) * softmax_scale
    main_scores = jnp.where(visible[:, None, :], main_scores, masked_fill)
    index_logits = contract_last(
        index_query.reshape(row_local * index_heads, index_width), index_keys
    )
    index_logits = index_logits.reshape(row_local, index_heads, key_local)
    active = jnp.maximum(index_logits, 0.0)
    index_scores = jnp.einsum("qj,qjk->qk", index_weight, active, precision=lax.Precision.HIGHEST)
    index_scores = jnp.where(row_visible, index_scores, masked_fill)
    main_local = jnp.max(main_scores, axis=2)
    index_local = jnp.max(index_scores, axis=1)
    main_maxima, index_maxima = lax.pmax((main_local, index_local), "keys")
    main_sum = jnp.sum(
        jnp.where(visible[:, None, :], jnp.exp(main_scores - main_maxima[:, :, None]), 0.0), axis=2
    )
    index_sum = jnp.sum(
        jnp.where(row_visible, jnp.exp(index_scores - index_maxima[:, None]), 0.0), axis=1
    )
    main_totals, index_totals = lax.psum((main_sum, index_sum), "keys")
    main_probs = (
        jnp.where(visible[:, None, :], jnp.exp(main_scores - main_maxima[:, :, None]), 0.0)
        / main_totals[:, :, None]
    )
    partial_value = jnp.sum(main_probs, axis=1)
    summed = lax.psum(partial_value, "heads")
    target = lax.dynamic_slice_in_dim(summed, row_first, row_local, 0)
    target = target / H
    index_probs = (
        jnp.where(row_visible, jnp.exp(index_scores - index_maxima[:, None]), 0.0)
        / index_totals[:, None]
    )
    index_delta = kl_weight[:, None] * (index_probs - target)
    weight_grad = jnp.einsum("qk,qjk->qj", index_delta, active, precision=lax.Precision.HIGHEST)
    slopes = jnp.where(
        index_logits > 0.0, index_delta[:, None, :] * index_weight[:, :, None], 0.0
    ).astype(jnp.bfloat16)
    flattened = slopes.reshape(row_local * index_heads, key_local)
    query_grad = jnp.dot(flattened, index_keys, preferred_element_type=jnp.float32).reshape(
        row_local, index_heads, index_width
    )
    key_grad = lax.dot_general(
        flattened,
        index_query.reshape(row_local * index_heads, index_width),
        (((0,), (0,)), ((), ())),
        preferred_element_type=jnp.float32,
    )
    query_grad, weight_grad = lax.psum((query_grad, weight_grad), "keys")
    key_grad = lax.psum(key_grad, "heads")
    return (query_grad, key_grad, weight_grad)


def solution(mesh):
    placed = (
        P(None, "heads", None),
        P("keys", None),
        P("heads", None, None),
        P("keys", None),
        P("heads", None),
        P(),
        P("heads"),
    )
    return jax.shard_map(
        shards,
        mesh=mesh,
        in_specs=placed,
        out_specs=(P("heads", None, None), P("keys", None), P("heads", None)),
        check_vma=False,
    )
```

profile of v0, /device:TPU:1, one launch (start us, length us, event | category | flops | bytes accessed | tf_op | source)
XLA Modules:
  0.0 565.1 jit_solution(11761084762094805328)
XLA Ops:
  7.2 0.0 copy-start
  7.2 0.0 copy-start.4
  7.2 0.0 all-reduce.6.cloned.1.call-start
  7.3 0.9 dynamic_slice.6
  8.2 0.0 copy-start.6
  8.2 1.0 broadcast_compare_fusion
  9.2 0.0 copy-start.8
  9.2 3.3 fusion.8
  12.5 0.0 copy-start.1
  12.6 3.2 copy-done.1
  15.8 0.0 copy-done.4
  15.8 4.6 fusion.4
  20.4 0.2 fusion.28
  20.6 0.0 copy-done
  20.6 0.0 copy-done.8
  20.6 11.6 %fusion = (f32[256,8]{0,1:T(8,128)S(1)}, f32[256,8,2048]{2,0,1:T(8,128)}) fusion(pred[256,2048]{1,0:T(8,128)(4,1)S(1)} %broadcast_compare_fusion, bf16[256,8,576]{0,2,1:T(8,128)(2,1)S(1)} %copy-done, bf16[2048,576]{0,1:T(8,128)(2,1)S(1)} %copy-done.8), kind=kOutput, calls=%fused_computation.3 | convolution fusion | flops 4844419072 | bytes 22028288 | tf_op jit(solution)/shard_map/dot_general | solution.py:12
  32.2 39.7 %all-reduce.1 = (f32[256,8]{0,1:T(8,128)S(1)}, f32[16]{0:T(128)S(1)}) all-reduce(f32[256,8]{0,1:T(8,128)S(1)} %get-tuple-element.7, f32[16]{0:T(128)S(1)} %fusion.28), channel_id=1, replica_groups=mesh['heads'=16,'keys'=16] {'keys'}, use_global_device_ids=true, to_apply=%region_5.6 | all-reduce | flops 2064 | bytes 16512 | tf_op jit(solution)/shard_map/pmax | solution.py:41
  71.9 0.0 copy-start.7
  71.9 0.0 copy-done.6
  71.9 0.2 fusion.29
  72.1 8.4 %fusion.1 = f32[256,8]{0,1:T(8,128)S(1)} fusion(f32[256,8,2048]{2,0,1:T(8,128)} %get-tuple-element.8, f32[256,8]{0,1:T(8,128)S(1)} %get-tuple-element.5, pred[256,2048]{1,0:T(8,128)(4,1)S(1)} %broadcast_compare_fusion), kind=kLoop, calls=%fused_computation.4 | loop fusion | flops 20969472 | bytes 17317888 | tf_op jit(solution)/shard_map/reduce_sum | solution.py:42
  80.5 0.0 copy-done.7
  80.5 31.6 %all-reduce = (f32[256,8]{0,1:T(8,128)}, f32[16]{0:T(128)}) all-reduce(f32[256,8]{0,1:T(8,128)S(1)} %fusion.1, f32[16]{0:T(128)S(1)} %fusion.29), channel_id=1, replica_groups=mesh['heads'=16,'keys'=16] {'keys'}, use_global_device_ids=true, to_apply=%region_7.8 | all-reduce | flops 2064 | bytes 16512 | tf_op jit(solution)/shard_map/psum | solution.py:48
  112.2 0.0 copy-start.2
  112.2 10.2 %divide_reduce_fusion = f32[256,2048]{1,0:T(8,128)} fusion(f32[256,8,2048]{2,0,1:T(8,128)} %get-tuple-element.8, f32[256,8]{0,1:T(8,128)} %get-tuple-element.3, f32[256,8]{0,1:T(8,128)S(1)} %get-tuple-element.5, pred[256,2048]{1,0:T(8,128)(4,1)S(1)} %broadcast_compare_fusion), kind=kLoop, calls=%fused_computation.2 | loop fusion | flops 24641536 | bytes 19415040 | tf_op jit(solution)/shard_map/reduce_sum | solution.py:53
  122.4 0.0 all-reduce.6.cloned.1.call-update
  122.4 0.0 all-reduce.8.cloned.1.call-start
  122.4 140.4 %all-reduce.6.cloned.1.call-done = f32[256,2048]{1,0:T(8,128)} async-done(((f32[256,2048]{1,0:T(8,128)}), f32[256,2048]{1,0:T(8,128)}) %all-reduce.6.cloned.1.call-update) | async-done | bytes 2097168 | tf_op jit(solution)/shard_map/psum | solution.py:54
  262.9 1.1 subtract_multiply_fusion
  263.9 0.0 copy-done.2
  264.0 0.0 copy-start.3
  264.0 0.0 copy-start.5
  264.0 3.1 fusion.7
  267.1 0.0 all-reduce.8.cloned.1.call-update
  267.1 0.0 all-reduce.10.cloned.1.call-start
  267.2 0.0 copy-done.3
  267.2 0.0 copy-done.5
  267.2 3.6 fusion.19
  270.8 0.0 all-reduce.10.cloned.1.call-update
  270.8 9.0 %fusion.2 = f32[16,1,64]{2,1,0:T(1,128)S(1)} fusion(f32[16,64,2048]{2,1,0:T(8,128)} %copy-done.1, f32[16,2048,1]{1,0,2:T(8,128)S(1)} %bitcast.34), kind=kOutput, calls=%fused_computation.8 | convolution fusion | flops 27262976 | bytes 8523776 | tf_op jit(solution)/shard_map/qk,qjk->qj/dot_general | solution.py:62
  279.8 36.5 %psum.47 = f32[16,64]{1,0:T(8,128)} all-reduce(f32[16,64]{1,0:T(8,128)S(1)} %bitcast.35), channel_id=1, replica_groups=mesh['heads'=16,'keys'=16] {'keys'}, use_global_device_ids=true, to_apply=%region_12.13 | all-reduce | flops 1024 | bytes 8192 | tf_op jit(solution)/shard_map/psum | solution.py:76
  316.4 100.5 %all-reduce.8.cloned.1.call-done = f32[16,64,128]{2,1,0:T(8,128)} async-done(((f32[16,64,128]{2,1,0:T(8,128)}), f32[16,64,128]{2,1,0:T(8,128)}) %all-reduce.8.cloned.1.call-update) | async-done | bytes 524304 | tf_op jit(solution)/shard_map/psum | solution.py:76
  416.9 137.6 %all-reduce.10.cloned.1.call-done = f32[2048,128]{1,0:T(8,128)} async-done(((f32[2048,128]{1,0:T(8,128)}), f32[2048,128]{1,0:T(8,128)}) %all-reduce.10.cloned.1.call-update) | async-done | bytes 1048592 | tf_op jit(solution)/shard_map/psum | solution.py:77
  554.5 1.9 copy.28
  556.3 2.3 copy.29
  (1 shorter events, 0.0 us)
Async XLA Ops:
  7.2 13.4 %copy-start = (bf16[256,8,576]{0,2,1:T(8,128)(2,1)S(1)}, bf16[256,8,576]{0,2,1:T(8,128)(2,1)}, u32[]{:S(2)}) copy-start(bf16[256,8,576]{0,2,1:T(8,128)(2,1)} %param.7) | copy-start | bytes 7077892
  7.2 8.6 %copy-start.4 = (f32[16,64]{1,0:T(8,128)S(1)}, f32[16,64]{1,0:T(8,128)}, u32[]{:S(2)}) copy-start(f32[16,64]{1,0:T(8,128)} %param.11) | copy-start | bytes 12292
  7.2 255.7 %all-reduce.6.cloned.1.call-start = ((), (), s32[]{:S(2)}) async-start(), calls=%async_computation | async-start | bytes 4194304 | tf_op jit(solution)/shard_map/psum | solution.py:54
  8.2 63.8 %copy-start.6 = (s32[16]{0:T(128)}, s32[16]{0:T(128)S(1)}, u32[]{:S(2)}) copy-start(s32[16]{0:T(128)S(1)} %dynamic_slice.6) | copy-start | bytes 196
  9.2 11.4 %copy-start.8 = (bf16[2048,576]{0,1:T(8,128)(2,1)S(1)}, bf16[2048,576]{0,1:T(8,128)(2,1)}, u32[]{:S(2)}) copy-start(bf16[2048,576]{0,1:T(8,128)(2,1)} %param.8) | copy-start | bytes 7077892
  12.5 3.2 copy-start.1
  71.9 8.6 %copy-start.7 = (f32[16]{0:T(128)}, f32[16]{0:T(128)S(1)}, u32[]{:S(2)}) copy-start(f32[16]{0:T(128)S(1)} %get-tuple-element.6) | copy-start | bytes 196
  112.2 151.8 %copy-start.2 = (bf16[2048,128]{1,0:T(8,128)(2,1)S(1)}, bf16[2048,128]{1,0:T(8,128)(2,1)}, u32[]{:S(2)}) copy-start(bf16[2048,128]{1,0:T(8,128)(2,1)} %param.10) | copy-start | bytes 1572868
  122.4 294.5 %all-reduce.8.cloned.1.call-start = ((), (), s32[]{:S(2)}) async-start(), calls=%async_computation.1 | async-start | bytes 1048576 | tf_op jit(solution)/shard_map/psum | solution.py:76
  264.0 3.2 copy-start.3
  264.0 3.2 copy-start.5
  267.1 287.3 %all-reduce.10.cloned.1.call-start = ((), (), s32[]{:S(2)}) async-start(), calls=%async_computation.2 | async-start | bytes 2097152 | tf_op jit(solution)/shard_map/psum | solution.py:77
Sparse Core Ops, SparseCore 0:
  122.5 140.3 all-reduce.5
  267.3 149.5 all-reduce.7
  420.1 134.3 all-reduce.9
where the time goes:
time: 566 us; the launch traced here: 565 us
  waiting for transfers between devices  379 us (67%)
  blocking collectives  108 us (19%)
  matrix products  35.3 us (6%)
  other arithmetic  21.1 us (4%)
  between operations  13.9 us (2%)
  local copies, waits for them, and re-layouts  8.32 us (1%)
    psum x1, waiting for transfers between devices, shards(): summed = lax.psum(partial_value, 'heads')  140 us
    psum x1, waiting for transfers between devices, shards(): key_grad = lax.psum(key_grad, 'heads')  138 us
    psum x1, waiting for transfers between devices, shards(): query_grad, weight_grad = lax.psum((query_grad, weight_grad), 'keys')  101 us
    pmax x1, blocking collectives, shards(): main_maxima, index_maxima = lax.pmax((main_local, index_local), 'keys')  39.7 us
    psum x1, blocking collectives, shards(): query_grad, weight_grad = lax.psum((query_grad, weight_grad), 'keys')  36.5 us
    psum x1, blocking collectives, shards(): main_totals, index_totals = lax.psum((main_sum, index_sum), 'keys')  31.6 us
    dot_general x2, matrix products, contract_last(): lax.dot_general(left_side, right_side, (((1,), (1,)), ((), ())), preferre...  15 us
  transfers between devices with their start and end apart: 3, of which 3 were waited for; matrix products, arithmetic and copies ran while one was open for 2% of the time, Pallas kernels for 0%

commit v1 on v0

--- a/solution.py
+++ b/solution.py
@@ -51,7 +51,7 @@
         / main_totals[:, :, None]
     )
     partial_value = jnp.sum(main_probs, axis=1)
-    summed = lax.psum(partial_value, "heads")
+    summed = jnp.sum(lax.all_gather(partial_value, "heads"), axis=0)
     target = lax.dynamic_slice_in_dim(summed, row_first, row_local, 0)
     target = target / H
     index_probs = (

time: 566 us -> 620 us (1.095)
  waiting for transfers between devices: 379 us -> 424 us
  other arithmetic: 21.1 us -> 32 us
    all_gather x0 -> x1, waiting for transfers between devices: none -> 186 us  [shards(): summed = jnp.sum(lax.all_gather(partial_value, 'heads'), axis=0)]
    psum x1 -> x0, waiting for transfers between devices: 140 us -> none  [shards(): summed = lax.psum(partial_value, 'heads')]
    reduce_sum x0 -> x1, other arithmetic: none -> 11.9 us  [shards(): summed = jnp.sum(lax.all_gather(partial_value, 'heads'), axis=0)]
where the time goes in v1:
time: 620 us
  waiting for transfers between devices  424 us (68%)
  blocking collectives  108 us (17%)
  matrix products  33.2 us (5%)
  other arithmetic  32 us (5%)
  between operations  14 us (2%)
  local copies, waits for them, and re-layouts  8.59 us (1%)
    all_gather x1, waiting for transfers between devices, shards(): summed = jnp.sum(lax.all_gather(partial_value, 'heads'), axis=0)  186 us
    psum x1, waiting for transfers between devices, shards(): key_grad = lax.psum(key_grad, 'heads')  138 us
    psum x1, waiting for transfers between devices, shards(): query_grad, weight_grad = lax.psum((query_grad, weight_grad), 'keys')  101 us
    pmax x1, blocking collectives, shards(): main_maxima, index_maxima = lax.pmax((main_local, index_local), 'keys')  39.7 us
    psum x1, blocking collectives, shards(): query_grad, weight_grad = lax.psum((query_grad, weight_grad), 'keys')  36.7 us
    psum x1, blocking collectives, shards(): main_totals, index_totals = lax.psum((main_sum, index_sum), 'keys')  31.5 us
    dot_general x2, matrix products, contract_last(): lax.dot_general(left_side, right_side, (((1,), (1,)), ((), ())), preferre...  14.9 us
  transfers between devices with their start and end apart: 3, of which 3 were waited for; matrix products, arithmetic and copies ran while one was open for 2% of the time, Pallas kernels for 0%

profile of v1, /device:TPU:1, one launch (start us, length us, event | category | flops | bytes accessed | tf_op | source)
XLA Modules:
  0.0 619.6 jit_solution(10360382922772073594)
XLA Ops:
  7.2 0.0 copy-start
  7.2 0.0 copy-start.7
  7.2 0.0 all-gather.3.cloned.1.call-start
  7.3 0.9 dynamic_slice.6
  8.2 0.0 copy-start.8
  8.2 1.0 broadcast_compare_fusion
  9.2 0.0 copy-start.14
  9.2 3.3 fusion.8
  12.5 0.0 copy-start.2
  12.5 3.2 copy-done.2
  15.7 0.0 copy-done.7
  15.7 4.6 fusion.4
  20.3 0.2 fusion.28
  20.5 0.0 copy-done
  20.5 0.0 copy-done.14
  20.5 11.6 %fusion = (f32[256,8]{0,1:T(8,128)S(1)}, f32[256,8,2048]{2,0,1:T(8,128)}) fusion(pred[256,2048]{1,0:T(8,128)(4,1)S(1)} %broadcast_compare_fusion, bf16[256,8,576]{0,2,1:T(8,128)(2,1)S(1)} %copy-done, bf16[2048,576]{0,1:T(8,128)(2,1)S(1)} %copy-done.14), kind=kOutput, calls=%fused_computation.3 | convolution fusion | flops 4844419072 | bytes 22028288 | tf_op jit(solution)/shard_map/dot_general | solution.py:12
  32.1 39.7 %all-reduce.1 = (f32[256,8]{0,1:T(8,128)S(1)}, f32[16]{0:T(128)S(1)}) all-reduce(f32[256,8]{0,1:T(8,128)S(1)} %get-tuple-element.7, f32[16]{0:T(128)S(1)} %fusion.28), channel_id=1, replica_groups=mesh['heads'=16,'keys'=16] {'keys'}, use_global_device_ids=true, to_apply=%region_5.6 | all-reduce | flops 2064 | bytes 16512 | tf_op jit(solution)/shard_map/pmax | solution.py:41
  71.8 0.0 copy-start.10
  71.9 0.0 copy-done.8
  71.9 0.2 fusion.29
  72.1 0.3 copy-done.10
  72.4 8.4 %fusion.1 = f32[256,8]{0,1:T(8,128)S(1)} fusion(f32[256,8,2048]{2,0,1:T(8,128)} %get-tuple-element.8, f32[256,8]{0,1:T(8,128)S(1)} %get-tuple-element.5, pred[256,2048]{1,0:T(8,128)(4,1)S(1)} %broadcast_compare_fusion), kind=kLoop, calls=%fused_computation.4 | loop fusion | flops 20969472 | bytes 17317888 | tf_op jit(solution)/shard_map/reduce_sum | solution.py:42
  80.7 31.5 %all-reduce = (f32[256,8]{0,1:T(8,128)S(1)}, f32[16]{0:T(128)}) all-reduce(f32[256,8]{0,1:T(8,128)S(1)} %fusion.1, f32[16]{0:T(128)S(1)} %fusion.29), channel_id=1, replica_groups=mesh['heads'=16,'keys'=16] {'keys'}, use_global_device_ids=true, to_apply=%region_7.8 | all-reduce | flops 2064 | bytes 16512 | tf_op jit(solution)/shard_map/psum | solution.py:48
  112.3 10.1 %divide_reduce_fusion = f32[256,2048]{1,0:T(8,128)} fusion(f32[256,8,2048]{2,0,1:T(8,128)} %get-tuple-element.8, f32[256,8]{0,1:T(8,128)S(1)} %get-tuple-element.3, f32[256,8]{0,1:T(8,128)S(1)} %get-tuple-element.5, pred[256,2048]{1,0:T(8,128)(4,1)S(1)} %broadcast_compare_fusion), kind=kLoop, calls=%fused_computation.2 | loop fusion | flops 24641536 | bytes 19415040 | tf_op jit(solution)/shard_map/reduce_sum | solution.py:53
  122.4 0.0 all-gather.3.cloned.1.call-update
  122.4 0.0 all-reduce.5.cloned.1.call-start
  122.5 185.6 %all-gather.3.cloned.1.call-done = f32[4096,2048]{1,0:T(8,128)} async-done(((f32[256,2048]{1,0:T(8,128)}), f32[4096,2048]{1,0:T(8,128)}) %all-gather.3.cloned.1.call-update) | async-done | bytes 33554448 | tf_op jit(solution)/shard_map/all_gather | solution.py:54
  308.1 0.0 copy-start.9
  308.1 0.0 copy-start.11
  308.1 0.0 copy-start.12
  308.1 0.0 copy-start.13
  308.1 0.0 copy-start.3
  308.1 0.0 copy-start.5
  308.1 11.9 %reduce_sum.39 = f32[256,2048]{1,0:T(8,128)S(1)} reduce(f32[16,256,2048]{2,1,0:T(8,128)} %bitcast.35, f32[]{:T(128)} %constant.11.clone.1), dimensions={0}, to_apply=%region_9.10 | reduce | flops 7864320 | bytes 35651588 | tf_op jit(solution)/shard_map/reduce_sum | solution.py:54
  320.0 0.0 copy-done.9
  320.0 0.0 copy-done.11
  320.1 0.0 copy-done.12
  320.1 0.0 copy-done.13
  320.1 0.1 subtract_multiply_fusion
  320.2 0.0 copy-done.3
  320.2 0.0 copy-done.5
  320.2 0.0 copy-start.4
  320.2 0.0 copy-start.6
  320.2 2.1 fusion.7
  322.3 0.0 all-reduce.5.cloned.1.call-update
  322.4 0.0 all-reduce.7.cloned.1.call-start
  322.4 0.0 copy-done.4
  322.4 0.0 copy-done.6
  322.4 0.0 copy-start.1
  322.5 2.6 fusion.19
  325.1 0.0 all-reduce.7.cloned.1.call-update
  325.1 9.0 %fusion.2 = f32[16,1,64]{2,1,0:T(1,128)S(1)} fusion(f32[16,64,2048]{2,1,0:T(8,128)} %copy-done.2, f32[16,2048,1]{1,0,2:T(8,128)S(1)} %bitcast.36), kind=kOutput, calls=%fused_computation.8 | convolution fusion | flops 27262976 | bytes 8523776 | tf_op jit(solution)/shard_map/qk,qjk->qj/dot_general | solution.py:62
  334.1 36.7 %psum.39 = f32[16,64]{1,0:T(8,128)} all-reduce(f32[16,64]{1,0:T(8,128)S(1)} %bitcast.37), channel_id=1, replica_groups=mesh['heads'=16,'keys'=16] {'keys'}, use_global_device_ids=true, to_apply=%region_12.13 | all-reduce | flops 1024 | bytes 8192 | tf_op jit(solution)/shard_map/psum | solution.py:76
  370.7 100.6 %all-reduce.5.cloned.1.call-done = f32[16,64,128]{2,1,0:T(8,128)} async-done(((f32[16,64,128]{2,1,0:T(8,128)}), f32[16,64,128]{2,1,0:T(8,128)}) %all-reduce.5.cloned.1.call-update) | async-done | bytes 524304 | tf_op jit(solution)/shard_map/psum | solution.py:76
  471.4 137.5 %all-reduce.7.cloned.1.call-done = f32[2048,128]{1,0:T(8,128)} async-done(((f32[2048,128]{1,0:T(8,128)}), f32[2048,128]{1,0:T(8,128)}) %all-reduce.7.cloned.1.call-update) | async-done | bytes 1048592 | tf_op jit(solution)/shard_map/psum | solution.py:77
  608.9 1.9 copy.27
  610.8 2.3 copy.28
  613.0 0.0 copy-done.1
  (1 shorter events, 0.0 us)
Async XLA Ops:
  7.2 13.4 %copy-start = (bf16[256,8,576]{0,2,1:T(8,128)(2,1)S(1)}, bf16[256,8,576]{0,2,1:T(8,128)(2,1)}, u32[]{:S(2)}) copy-start(bf16[256,8,576]{0,2,1:T(8,128)(2,1)} %param.7) | copy-start | bytes 7077892
  7.2 8.5 %copy-start.7 = (f32[16,64]{1,0:T(8,128)S(1)}, f32[16,64]{1,0:T(8,128)}, u32[]{:S(2)}) copy-start(f32[16,64]{1,0:T(8,128)} %param.11) | copy-start | bytes 12292
  7.2 300.9 %all-gather.3.cloned.1.call-start = ((), (), s32[]{:S(2)}) async-start(), calls=%async_computation.2 | async-start | bytes 35651584 | tf_op jit(solution)/shard_map/all_gather | solution.py:54
  8.2 63.7 %copy-start.8 = (s32[16]{0:T(128)}, s32[16]{0:T(128)S(1)}, u32[]{:S(2)}) copy-start(s32[16]{0:T(128)S(1)} %dynamic_slice.6) | copy-start | bytes 196
  9.2 11.3 %copy-start.14 = (bf16[2048,576]{0,1:T(8,128)(2,1)S(1)}, bf16[2048,576]{0,1:T(8,128)(2,1)}, u32[]{:S(2)}) copy-start(bf16[2048,576]{0,1:T(8,128)(2,1)} %param.8) | copy-start | bytes 7077892
  12.5 3.2 copy-start.2
  71.8 0.5 copy-start.10
  122.4 348.9 %all-reduce.5.cloned.1.call-start = ((), (), s32[]{:S(2)}) async-start(), calls=%async_computation | async-start | bytes 1048576 | tf_op jit(solution)/shard_map/psum | solution.py:76
  308.1 11.9 %copy-start.9 = (s32[16]{0:T(128)S(1)}, s32[16]{0:T(128)}, u32[]{:S(2)}) copy-start(s32[16]{0:T(128)} %copy-done.8) | copy-start | bytes 196
  308.1 11.9 %copy-start.11 = (f32[16]{0:T(128)S(1)}, f32[16]{0:T(128)}, u32[]{:S(2)}) copy-start(f32[16]{0:T(128)} %copy-done.10) | copy-start | bytes 196
  308.1 11.9 %copy-start.12 = (f32[16]{0:T(128)S(1)}, f32[16]{0:T(128)}, u32[]{:S(2)}) copy-start(f32[16]{0:T(128)} %param.13) | copy-start | bytes 196
  308.1 12.0 %copy-start.13 = (f32[16]{0:T(128)S(1)}, f32[16]{0:T(128)}, u32[]{:S(2)}) copy-start(f32[16]{0:T(128)} %get-tuple-element.4) | copy-start | bytes 196
  308.1 12.1 %copy-start.3 = (bf16[2048,128]{1,0:T(8,128)(2,1)S(1)}, bf16[2048,128]{1,0:T(8,128)(2,1)}, u32[]{:S(2)}) copy-start(bf16[2048,128]{1,0:T(8,128)(2,1)} %param.10) | copy-start | bytes 1572868
  308.1 12.1 %copy-start.5 = (u16[64,2048]{1,0:T(8,128)(2,1)S(1)}, u16[64,2048]{1,0:T(8,128)(2,1)}, u32[]{:S(2)}) copy-start(u16[64,2048]{1,0:T(8,128)(2,1)} %get-tuple-element.9) | copy-start | bytes 786436
  320.2 2.2 copy-start.4
  320.2 2.2 copy-start.6
  322.4 286.5 %all-reduce.7.cloned.1.call-start = ((), (), s32[]{:S(2)}) async-start(), calls=%async_computation.1 | async-start | bytes 2097152 | tf_op jit(solution)/shard_map/psum | solution.py:77
  322.4 290.6 %copy-start.1 = (bf16[256,8,576]{0,2,1:T(8,128)(2,1)S(1)}, bf16[256,8,576]{0,2,1:T(8,128)(2,1)}, u32[]{:S(2)}) copy-start(bf16[256,8,576]{0,2,1:T(8,128)(2,1)} %param.7) | copy-start | bytes 7077892
Sparse Core Ops, SparseCore 0:
  122.6 185.4 all-gather.2
  322.5 148.8 all-reduce.4
  474.6 134.2 all-reduce.6
